TPU v7x, 32 devices: a whole 2x2x4 slice. The times are simulated.
32 devices in a mesh: slab: 8 (over z, core), dom: 4 (over y, x).
Axes of the slice: x: 2, y: 2, z: 4, core: 2. Of those that a mesh axis runs over, the one named last changes fastest.
Arguments:
- positions: float32 [3, 16384], P(None, ('slab', 'dom')), may hold values from -0.5 to 32.5, as said below
- burgers: float32 [3, 16384], P(None, ('slab', 'dom')), may hold values from -6 to 6
- mobility: float32 [16384], P(('slab', 'dom')), may hold values from 0.5 to 2
- block_cells: int32 [128], P(('slab', 'dom')), may hold values from 0 to 127, as said below
- pairs: int32 [2048, 2], P(('slab', 'dom')), may hold values from 0 to 127, as said below
- pair_count: int32 [32], P(('slab', 'dom')), may hold values from 8 to 64, as said below
Outputs:
- moved: float32 [3, 16384], P(None, ('slab', 'dom'))
- velocity: float32 [3, 16384], P(None, ('slab', 'dom'))
Inputs may be any that keep to these rules, and one draw needn't show every extreme that they name: `block_cells`: block k lies in slab k // (4 * 4) and its cell is 16 times that slab plus 0 to 15. `positions`: each segment lies within 2.5 of its block's cell centre along x and within 1.5 along y and z. `pairs`: device d = s * 4 + e owns blocks d * 4 to (d + 1) * 4 - 1. In device d's slots the first block is one of its own; the second is owned by a device of slab s - 1, s or s + 1 at dom position e - 1, e or e + 1, and differs from the first. Every slot holds such a pair, used or not. `pair_count`: in each slab exactly one device has 64 used slots; the others have at most 32.
All inputs are finite; a program needn't handle non-finite values.
Results may differ from a plain program's by a relative error of at most 0.0003.
Values sent between devices are 32-bit elements; how exact they have to be, the bound alone decides.
No kernel may reach another device: no remote copies, remote signals or barrier semaphores. Data moves between devices by JAX's collectives and lax.ppermute only.
A program may use at most 64 MiB of HBM per device.

v0:
```python
import math
import jax
import jax.numpy as jnp
from jax import lax
from jax.sharding import PartitionSpec as P

BLOCK_SEGS = 128
core_near = 0.25
core_far = 9.0
time_increment = 0.25
pair_batch = 4
hi_prec = lax.Precision.HIGHEST


def padded(x, sides, width):
    for axis, dim in sides:
        peers, length = (lax.axis_size(axis), x.shape[dim])
        up = [(i, (i + 1) % peers) for i in range(peers - 1)]
        down = [(j, i) for i, j in up]
        last = lax.slice_in_dim(x, length - width, length, axis=dim)
        initial = lax.slice_in_dim(x, 0, width, axis=dim)
        before = lax.ppermute(last, axis, up)
        after = lax.ppermute(initial, axis, down)
        x = jnp.concatenate([before, x, after], axis=dim)
    return x


def shifted(block, axis, distance):
    devices = range(lax.axis_size(axis))
    route = [(i - distance, i) for i in devices if i - distance in devices]
    return lax.ppermute(block, axis, route)


def centers(cells):
    slabs = cells // 16
    rest = cells % 16
    return jnp.stack([4 * slabs + 2, 2 * (rest // 4) + 1, 2 * (rest % 4) + 1]).astype(jnp.float32)


def block_moments(posit, burg, cells, ncells, width, base_cell):
    nblk = cells.shape[0]
    offset = posit.reshape(3, nblk, width) - centers(cells)[:, :, None]
    vec = burg.reshape(3, nblk, width)
    first = (vec[:, None] * offset[None]).reshape(9, nblk, width)
    second = (vec[:, None, None] * offset[None, :, None] * offset[None, None, :]).reshape(
        27, nblk, width
    )
    rows = jnp.sum(jnp.concatenate([vec, first, second], axis=0), axis=2)
    onehot = ((cells - base_cell)[:, None] == jnp.arange(ncells, dtype=jnp.int32)[None, :]).astype(
        jnp.float32
    )
    return jnp.dot(rows, onehot, precision=hi_prec)


def far_field(posit, burg, moments):
    ncells = moments.shape[1]
    nblk = ncells // 64
    zeds = centers(jnp.arange(ncells, dtype=jnp.int32)).reshape(3, nblk, 64).transpose(1, 0, 2)
    mblk = moments.reshape(39, nblk, 64).transpose(1, 0, 2)

    def visit(acc, item):
        zpart, mpart = item
        r = posit[:, None, :] - zpart[:, :, None]
        sq = r[0] * r[0] + r[1] * r[1] + r[2] * r[2] + core_far
        inv3 = 1.0 / (sq * jnp.sqrt(sq))
        inv5 = inv3 / sq
        inv7 = inv5 / sq
        qzero = jnp.einsum("kc,kn->cn", mpart[0:3], burg, precision=hi_prec)
        qone = jnp.einsum("kac,kn->acn", mpart[3:12].reshape(3, 3, 64), burg, precision=hi_prec)
        qtwo = jnp.einsum(
            "kabc,kn->abcn", mpart[12:39].reshape(3, 3, 3, 64), burg, precision=hi_prec
        )
        qone_r = jnp.sum(qone * r, axis=0)
        qtwo_r = jnp.sum(qtwo * r[None], axis=1)
        rqr = jnp.sum(r * qtwo_r, axis=0)
        trace = qtwo[0, 0] + qtwo[1, 1] + qtwo[2, 2]
        scal = qzero * inv3 + 3.0 * qone_r * inv5 - 1.5 * trace * inv5 + 7.5 * rqr * inv7
        force = r * scal[None] - qone * inv3[None] - 3.0 * qtwo_r * inv5[None]
        return (acc + jnp.sum(force, axis=1), None)

    start = jnp.zeros(posit.shape, jnp.float32)
    total, unused = lax.scan(visit, start, (zeds, mblk))
    return total


def pair_forces(pos_a, bur_a, pos_b, bur_b, weight):
    r = pos_a[:, :, :, None] - pos_b[:, :, None, :]
    sq = r[0] * r[0] + r[1] * r[1] + r[2] * r[2]
    near_s = sq + core_near
    far_s = sq + core_far
    kern = 1.0 / (near_s * jnp.sqrt(near_s)) - 1.0 / (far_s * jnp.sqrt(far_s))
    coef = jnp.sum(bur_a[:, :, :, None] * bur_b[:, :, None, :], axis=0)
    wgt = weight[:, None, None] * coef * kern
    wr = wgt[None] * r
    return (jnp.sum(wr, axis=3), -jnp.sum(wr, axis=2))


def around_all(stacked):
    grown = padded(stacked[:, None, None, :], (("slab", 1), ("dom", 2)), 1)
    return grown.reshape(stacked.shape[0], -1)


def give_around(window_force, per_dev):
    grid = window_force.reshape(3, 3, 3, per_dev)
    from_above = shifted(grid[:, 0], "slab", -1)
    from_below = shifted(grid[:, 2], "slab", 1)
    row = grid[:, 1] + from_above + from_below
    from_right = shifted(row[:, 0], "dom", -1)
    from_left = shifted(row[:, 2], "dom", 1)
    return row[:, 1] + from_right + from_left


def body(positions, burgers, mobility, block_cells, pairs, pair_count):
    count_segs = positions.shape[1]
    width = BLOCK_SEGS
    n_slab = lax.axis_size("slab")
    n_dom = lax.axis_size("dom")
    ncells = 16 * n_slab
    blk_dev = block_cells.shape[0]
    far_scale = math.sqrt(ncells / (count_segs * n_slab * n_dom))
    slots = pairs.shape[0]
    my_slab = lax.axis_index("slab")
    my_dom = lax.axis_index("dom")
    used = pair_count[0]

    def locate(rotation_slots):
        return pairs[jnp.minimum(rotation_slots, slots - 1)]

    def to_window(blocks):
        owner = blocks // blk_dev
        within = blocks % blk_dev
        row_off = owner // n_dom - my_slab + 1
        col_off = owner % n_dom - my_dom + 1
        return jnp.clip((row_off * 3 + col_off) * blk_dev + within, 0, 9 * blk_dev - 1)

    def near(window):
        pos_win = window[0:3].reshape(3, -1, width)
        bur_win = window[3:6].reshape(3, -1, width)

        def turn(index, acc):
            rotation_slots = index * pair_batch + jnp.arange(pair_batch, dtype=jnp.int32)
            weight = (rotation_slots < used).astype(jnp.float32)
            chosen = locate(rotation_slots)
            first_blk = to_window(chosen[:, 0])
            second_blk = to_window(chosen[:, 1])
            force_a, force_b = pair_forces(
                pos_win[:, first_blk],
                bur_win[:, first_blk],
                pos_win[:, second_blk],
                bur_win[:, second_blk],
                weight,
            )
            return acc.at[:, first_blk].add(force_a).at[:, second_blk].add(force_b)

        groups = (used + pair_batch - 1) // pair_batch
        start = jnp.zeros(pos_win.shape, jnp.float32)
        return lax.fori_loop(0, groups, turn, start).reshape(3, -1)

    def gather_moments(posit):
        local = block_moments(posit, burgers, block_cells, 16, width, 16 * my_slab)
        summed = lax.psum(local, "dom")
        return lax.all_gather(summed, "slab", axis=1, tiled=True)

    def speed(posit, window):
        moments = gather_moments(posit)
        far = far_field(posit, burgers, moments)
        near_own = give_around(near(window), count_segs)
        return mobility[None, :] * (far_scale * far + near_own)

    stacked = jnp.concatenate([positions, burgers], axis=0)
    leading_window = around_all(stacked)
    first_v = speed(positions, leading_window)
    stepped = positions + time_increment * first_v
    restacked = jnp.concatenate([stepped, burgers], axis=0)
    window_second = around_all(restacked)
    second_v = speed(stepped, window_second)
    total = first_v + second_v
    return (positions + 0.5 * time_increment * total, 0.5 * total)


def solution(mesh):
    placed = (
        P(None, ("slab", "dom")),
        P(None, ("slab", "dom")),
        P(("slab", "dom")),
        P(("slab", "dom")),
        P(("slab", "dom"), None),
        P(("slab", "dom")),
    )
    return jax.shard_map(
        body,
        mesh=mesh,
        in_specs=placed,
        out_specs=(P(None, ("slab", "dom")), P(None, ("slab", "dom"))),
        check_vma=False,
    )
```

profile of v0, /device:TPU:0, one launch (start us, length us, event | category | flops | bytes accessed | tf_op | source)
XLA Modules:
  0.0 326.1 jit_solution(1120146685088651747)
XLA Ops:
  1.4 1.3 collective-permute-start.1
  2.6 3.0 collective-permute-start
  8.4 1.3 collective-permute-start.3
  9.7 5.5 %collective-permute-start.2 = (f32[6,3,1,512]{3,0,2,1:T(8,128)S(1)}, f32[6,3,1,512]{3,0,2,1:T(8,128)S(1)}, u32[]{:S(2)}, u32[]{:S(2)}) collective-permute-start(f32[6,3,1,512]{3,0,2,1:T(8,128)S(1)} %pad_maximum_fusion.4), channel_id=1, source_target_pairs={{0,1},{1,2},{2,3},{4,5},{5,6},{6,7},{8,9},{9,10},{10,11},{12,13},{... | collective-permute-start | bytes 110600 | tf_op jit(solution)/shard_map/ppermute | solution.py:22
  17.0 105.3 %while.48 = (s32[]{:T(128)}, f32[3,36,128]{2,0,1:T(4,128)S(1)}, s32[]{:T(128)}, s32[64,2]{1,0:T(8,128)S(1)}, s32[]{:T(128)}, /*index=5*/s32[]{:T(128)}, s32[]{:T...) while((s32[]{:T(128)}, f32[3,36,128]{2,0,1:T(4,128)S(1)}, ...), condition=%wide.region_14.15_spmd, body=%wide.region_8.14_spmd.sunk | while | flops 2233267 | bytes 2855389 | solution.py:157
  122.3 1.3 collective-permute-start.4
  123.6 3.0 collective-permute-start.5
  126.7 11.5 %psum.14 = f32[39,16]{0,1:T(8,128)S(1)} all-reduce(f32[39,16]{0,1:T(8,128)S(1)} %fusion.151), channel_id=1, replica_groups=mesh['slab'=8,'dom'=4] {'dom'}, use_global_device_ids=true, to_apply=%region_1.2 | all-reduce | flops 624 | bytes 4992 | tf_op jit(solution)/shard_map/psum | solution.py:161
  138.2 14.7 %all_gather.6 = f32[39,128]{0,1:T(8,128)S(1)} all-gather(f32[39,16]{0,1:T(8,128)S(1)} %psum.14), channel_id=1, replica_groups=mesh['slab'=8,'dom'=4] {'slab'}, dimensions={1}, use_global_device_ids=true | all-gather | bytes 22464 | tf_op jit(solution)/shard_map/all_gather | solution.py:162
  153.0 1.3 collective-permute-start.6
  154.3 4.5 %collective-permute-start.7 = (f32[3,512]{1,0:T(4,128)S(1)}, f32[3,512]{1,0:T(4,128)S(1)}, u32[]{:S(2)}, u32[]{:S(2)}) collective-permute-start(f32[3,512]{1,0:T(4,128)S(1)} %get-tuple-element.575), channel_id=1, source_target_pairs={{0,1},{1,2},{2,3},{4,5},{5,6},{6,7},{8,9},{9,10},{10,11},{12,13},{... | collective-permute-start | bytes 18440 | tf_op jit(solution)/shard_map/ppermute | solution.py:31
  158.9 5.3 %while.50 = (s32[]{:T(128)}, f32[3,512]{1,0:T(4,128)S(1)}, f32[3,512]{1,0:T(4,128)S(1)}, f32[2,3,64]{2,1,0:T(4,128)S(1)}, f32[2,39,64]{2,1,0:T(8,128)S(1)}, /*in...) while((s32[]{:T(128)}, f32[3,512]{1,0:T(4,128)S(1)}, f32[3,512]{1,0:T(4,128)S(1)}, ...), condition=%wide.region_7.8_spmd.clone, body=%wide.region_2.7_spmd.clone.sunk | while | flops 18023940 | bytes 6538151 | solution.py:82
  164.3 1.3 collective-permute-start.9
  165.6 3.0 collective-permute-start.8
  170.7 4.5 %collective-permute-start.10 = (f32[6,3,1,512]{3,0,2,1:T(8,128)S(1)}, f32[6,3,1,512]{3,0,2,1:T(8,128)S(1)}, u32[]{:S(2)}, u32[]{:S(2)}) collective-permute-start(f32[6,3,1,512]{3,0,2,1:T(8,128)S(1)} %pad_maximum_fusion.5), channel_id=1, source_target_pairs={{0,1},{1,2},{2,3},{4,5},{5,6},{6,7},{8,9},{9,10},{10,11},{12,13},{... | collective-permute-start | bytes 110600 | tf_op jit(solution)/shard_map/ppermute | solution.py:22
  175.6 1.7 collective-permute-done.10
  177.4 105.3 %while.49 = (s32[]{:T(128)}, f32[3,36,128]{2,0,1:T(4,128)S(1)}, s32[]{:T(128)}, s32[64,2]{1,0:T(8,128)S(1)}, s32[]{:T(128)}, /*index=5*/s32[]{:T(128)}, s32[]{:T...) while((s32[]{:T(128)}, f32[3,36,128]{2,0,1:T(4,128)S(1)}, ...), condition=%wide.region_29.30_spmd, body=%wide.region_23.29_spmd.sunk | while | flops 2233267 | bytes 2855389 | solution.py:157
  282.7 1.3 collective-permute-start.12
  284.0 3.0 collective-permute-start.13
  287.3 10.0 %psum.15 = f32[39,16]{0,1:T(8,128)S(1)} all-reduce(f32[39,16]{0,1:T(8,128)S(1)} %fusion.150), channel_id=1, replica_groups=mesh['slab'=8,'dom'=4] {'dom'}, use_global_device_ids=true, to_apply=%region_16.17 | all-reduce | flops 624 | bytes 4992 | tf_op jit(solution)/shard_map/psum | solution.py:161
  297.3 16.3 %all_gather.7 = f32[39,128]{0,1:T(8,128)S(1)} all-gather(f32[39,16]{0,1:T(8,128)S(1)} %psum.15), channel_id=1, replica_groups=mesh['slab'=8,'dom'=4] {'slab'}, dimensions={1}, use_global_device_ids=true | all-gather | bytes 22464 | tf_op jit(solution)/shard_map/all_gather | solution.py:162
  313.7 1.3 collective-permute-start.14
  315.0 4.5 %collective-permute-start.15 = (f32[3,512]{1,0:T(4,128)S(1)}, f32[3,512]{1,0:T(4,128)S(1)}, u32[]{:S(2)}, u32[]{:S(2)}) collective-permute-start(f32[3,512]{1,0:T(4,128)S(1)} %get-tuple-element.573), channel_id=1, source_target_pairs={{0,1},{1,2},{2,3},{4,5},{5,6},{6,7},{8,9},{9,10},{10,11},{12,13},{... | collective-permute-start | bytes 18440 | tf_op jit(solution)/shard_map/ppermute | solution.py:31
  319.5 5.3 %while.51 = (s32[]{:T(128)}, f32[3,512]{1,0:T(4,128)S(1)}, f32[3,512]{1,0:T(4,128)S(1)}, f32[2,3,64]{2,1,0:T(4,128)S(1)}, f32[2,39,64]{2,1,0:T(8,128)S(1)}, /*in...) while((s32[]{:T(128)}, f32[3,512]{1,0:T(4,128)S(1)}, f32[3,512]{1,0:T(4,128)S(1)}, ...), condition=%wide.region_22.23_spmd.clone, body=%wide.region_17.22_spmd.clone.sunk | while | flops 18023940 | bytes 6538151 | solution.py:82
  (854 shorter events, 226.7 us)
Async XLA Ops:
  1.4 7.0 %collective-permute-start.1 = (f32[6,1,1,512]{3,0,2,1:T(8,128)S(1)}, f32[6,1,1,512]{3,0,2,1:T(8,128)S(1)}, u32[]{:S(2)}, u32[]{:S(2)}) collective-permute-start(f32[6,1,1,512]{3,0,2,1:T(8,128)S(1)} %fusion.138), channel_id=1, source_target_pairs={{4,0},{8,4},{12,8},{16,12},{20,16},{24,20},{28,24},{5,1},{9,5},{13... | collective-permute-start | bytes 36872 | tf_op jit(solution)/shard_map/ppermute | solution.py:23
  2.6 5.7 %collective-permute-start = (f32[6,1,1,512]{3,0,2,1:T(8,128)S(1)}, f32[6,1,1,512]{3,0,2,1:T(8,128)S(1)}, u32[]{:S(2)}, u32[]{:S(2)}) collective-permute-start(f32[6,1,1,512]{3,0,2,1:T(8,128)S(1)} %fusion.138), channel_id=1, source_target_pairs={{0,4},{4,8},{8,12},{12,16},{16,20},{20,24},{24,28},{1,5},{5,9},{9,... | collective-permute-start | bytes 36872 | tf_op jit(solution)/shard_map/ppermute | solution.py:22
  8.4 8.3 %collective-permute-start.3 = (f32[6,3,1,512]{3,0,2,1:T(8,128)S(1)}, f32[6,3,1,512]{3,0,2,1:T(8,128)S(1)}, u32[]{:S(2)}, u32[]{:S(2)}) collective-permute-start(f32[6,3,1,512]{3,0,2,1:T(8,128)S(1)} %pad_maximum_fusion.4), channel_id=1, source_target_pairs={{1,0},{2,1},{3,2},{5,4},{6,5},{7,6},{9,8},{10,9},{11,10},{13,12},{... | collective-permute-start | bytes 110600 | tf_op jit(solution)/shard_map/ppermute | solution.py:23
  9.7 7.2 %collective-permute-start.2 = (f32[6,3,1,512]{3,0,2,1:T(8,128)S(1)}, f32[6,3,1,512]{3,0,2,1:T(8,128)S(1)}, u32[]{:S(2)}, u32[]{:S(2)}) collective-permute-start(f32[6,3,1,512]{3,0,2,1:T(8,128)S(1)} %pad_maximum_fusion.4), channel_id=1, source_target_pairs={{0,1},{1,2},{2,3},{4,5},{5,6},{6,7},{8,9},{9,10},{10,11},{12,13},{... | collective-permute-start | bytes 110600 | tf_op jit(solution)/shard_map/ppermute | solution.py:22
  17.0 141.9 %copy-start = (f32[3,512]{1,0:T(4,128)S(1)}, f32[3,512]{1,0:T(4,128)}, u32[]{:S(2)}) copy-start(f32[3,512]{1,0:T(4,128)} %param.15) | copy-start | bytes 18436
  17.0 141.9 %copy-start.1 = (f32[3,512]{1,0:T(4,128)S(1)}, f32[3,512]{1,0:T(4,128)}, u32[]{:S(2)}) copy-start(f32[3,512]{1,0:T(4,128)} %param.14) | copy-start | bytes 18436
  122.3 30.6 %collective-permute-start.4 = (f32[3,3,512]{2,0,1:T(4,128)S(1)}, f32[3,3,512]{2,0,1:T(4,128)S(1)}, u32[]{:S(2)}, u32[]{:S(2)}) collective-permute-start(f32[3,3,512]{2,0,1:T(4,128)S(1)} %get-tuple-element.570), channel_id=1, source_target_pairs={{4,0},{8,4},{12,8},{16,12},{20,16},{24,20},{28,24},{5,1},{9,5},{13... | collective-permute-start | bytes 55304 | tf_op jit(solution)/shard_map/ppermute | solution.py:31
  123.6 29.3 %collective-permute-start.5 = (f32[3,3,512]{2,0,1:T(4,128)S(1)}, f32[3,3,512]{2,0,1:T(4,128)S(1)}, u32[]{:S(2)}, u32[]{:S(2)}) collective-permute-start(f32[3,3,512]{2,0,1:T(4,128)S(1)} %get-tuple-element.571), channel_id=1, source_target_pairs={{0,4},{4,8},{8,12},{12,16},{16,20},{20,24},{24,28},{1,5},{5,9},{9,... | collective-permute-start | bytes 55304 | tf_op jit(solution)/shard_map/ppermute | solution.py:31
  153.0 11.2 %collective-permute-start.6 = (f32[3,512]{1,0:T(4,128)S(1)}, f32[3,512]{1,0:T(4,128)S(1)}, u32[]{:S(2)}, u32[]{:S(2)}) collective-permute-start(f32[3,512]{1,0:T(4,128)S(1)} %get-tuple-element.574), channel_id=1, source_target_pairs={{1,0},{2,1},{3,2},{5,4},{6,5},{7,6},{9,8},{10,9},{11,10},{13,12},{... | collective-permute-start | bytes 18440 | tf_op jit(solution)/shard_map/ppermute | solution.py:31
  154.3 9.9 %collective-permute-start.7 = (f32[3,512]{1,0:T(4,128)S(1)}, f32[3,512]{1,0:T(4,128)S(1)}, u32[]{:S(2)}, u32[]{:S(2)}) collective-permute-start(f32[3,512]{1,0:T(4,128)S(1)} %get-tuple-element.575), channel_id=1, source_target_pairs={{0,1},{1,2},{2,3},{4,5},{5,6},{6,7},{8,9},{9,10},{10,11},{12,13},{... | collective-permute-start | bytes 18440 | tf_op jit(solution)/shard_map/ppermute | solution.py:31
  158.8 5.4 %copy-start.2 = (f32[512]{0:T(512)S(1)}, f32[512]{0:T(512)}, u32[]{:S(2)}) copy-start(f32[512]{0:T(512)} %param.16) | copy-start | bytes 6148
  164.3 4.4 %collective-permute-start.9 = (f32[6,1,1,512]{3,0,2,1:T(8,128)S(1)}, f32[6,1,1,512]{3,0,2,1:T(8,128)S(1)}, u32[]{:S(2)}, u32[]{:S(2)}) collective-permute-start(f32[6,1,1,512]{3,0,2,1:T(8,128)S(1)} %fusion.139), channel_id=1, source_target_pairs={{4,0},{8,4},{12,8},{16,12},{20,16},{24,20},{28,24},{5,1},{9,5},{13... | collective-permute-start | bytes 36872 | tf_op jit(solution)/shard_map/ppermute | solution.py:23
  165.6 3.9 %collective-permute-start.8 = (f32[6,1,1,512]{3,0,2,1:T(8,128)S(1)}, f32[6,1,1,512]{3,0,2,1:T(8,128)S(1)}, u32[]{:S(2)}, u32[]{:S(2)}) collective-permute-start(f32[6,1,1,512]{3,0,2,1:T(8,128)S(1)} %fusion.139), channel_id=1, source_target_pairs={{0,4},{4,8},{8,12},{12,16},{16,20},{20,24},{24,28},{1,5},{5,9},{9,... | collective-permute-start | bytes 36872 | tf_op jit(solution)/shard_map/ppermute | solution.py:22
  169.4 6.1 %collective-permute-start.11 = (f32[6,3,1,512]{3,0,2,1:T(8,128)S(1)}, f32[6,3,1,512]{3,0,2,1:T(8,128)S(1)}, u32[]{:S(2)}, u32[]{:S(2)}) collective-permute-start(f32[6,3,1,512]{3,0,2,1:T(8,128)S(1)} %pad_maximum_fusion.5), channel_id=1, source_target_pairs={{1,0},{2,1},{3,2},{5,4},{6,5},{7,6},{9,8},{10,9},{11,10},{13,12},{... | collective-permute-start | bytes 110600 | tf_op jit(solution)/shard_map/ppermute | solution.py:23
  170.7 6.6 %collective-permute-start.10 = (f32[6,3,1,512]{3,0,2,1:T(8,128)S(1)}, f32[6,3,1,512]{3,0,2,1:T(8,128)S(1)}, u32[]{:S(2)}, u32[]{:S(2)}) collective-permute-start(f32[6,3,1,512]{3,0,2,1:T(8,128)S(1)} %pad_maximum_fusion.5), channel_id=1, source_target_pairs={{0,1},{1,2},{2,3},{4,5},{5,6},{6,7},{8,9},{9,10},{10,11},{12,13},{... | collective-permute-start | bytes 110600 | tf_op jit(solution)/shard_map/ppermute | solution.py:22
  282.7 30.9 %collective-permute-start.12 = (f32[3,3,512]{2,0,1:T(4,128)S(1)}, f32[3,3,512]{2,0,1:T(4,128)S(1)}, u32[]{:S(2)}, u32[]{:S(2)}) collective-permute-start(f32[3,3,512]{2,0,1:T(4,128)S(1)} %get-tuple-element.568), channel_id=1, source_target_pairs={{4,0},{8,4},{12,8},{16,12},{20,16},{24,20},{28,24},{5,1},{9,5},{13... | collective-permute-start | bytes 55304 | tf_op jit(solution)/shard_map/ppermute | solution.py:31
  284.0 29.6 %collective-permute-start.13 = (f32[3,3,512]{2,0,1:T(4,128)S(1)}, f32[3,3,512]{2,0,1:T(4,128)S(1)}, u32[]{:S(2)}, u32[]{:S(2)}) collective-permute-start(f32[3,3,512]{2,0,1:T(4,128)S(1)} %get-tuple-element.569), channel_id=1, source_target_pairs={{0,4},{4,8},{8,12},{12,16},{16,20},{20,24},{24,28},{1,5},{5,9},{9,... | collective-permute-start | bytes 55304 | tf_op jit(solution)/shard_map/ppermute | solution.py:31
  313.7 11.2 %collective-permute-start.14 = (f32[3,512]{1,0:T(4,128)S(1)}, f32[3,512]{1,0:T(4,128)S(1)}, u32[]{:S(2)}, u32[]{:S(2)}) collective-permute-start(f32[3,512]{1,0:T(4,128)S(1)} %get-tuple-element.572), channel_id=1, source_target_pairs={{1,0},{2,1},{3,2},{5,4},{6,5},{7,6},{9,8},{10,9},{11,10},{13,12},{... | collective-permute-start | bytes 18440 | tf_op jit(solution)/shard_map/ppermute | solution.py:31
  315.0 9.9 %collective-permute-start.15 = (f32[3,512]{1,0:T(4,128)S(1)}, f32[3,512]{1,0:T(4,128)S(1)}, u32[]{:S(2)}, u32[]{:S(2)}) collective-permute-start(f32[3,512]{1,0:T(4,128)S(1)} %get-tuple-element.573), channel_id=1, source_target_pairs={{0,1},{1,2},{2,3},{4,5},{5,6},{6,7},{8,9},{9,10},{10,11},{12,13},{... | collective-permute-start | bytes 18440 | tf_op jit(solution)/shard_map/ppermute | solution.py:31
where the time goes:
time: 327 us; the launch traced here: 326 us
  other arithmetic  121 us (37%)
  local copies, waits for them, and re-layouts  94.8 us (29%)
  blocking collectives  52.4 us (16%)
  starting transfers between devices  41.6 us (13%)
  matrix products  8.84 us (3%)
    scatter-add x64, other arithmetic, turn(): return acc.at[:, first_blk].add(force_a).at[:, second_blk].add(force_b)  41.4 us
    all_gather x2, blocking collectives, gather_moments(): return lax.all_gather(summed, 'slab', axis=1, tiled=True)  30.9 us
    psum x2, blocking collectives, gather_moments(): summed = lax.psum(local, 'dom')  21.4 us
    convert_element_type x32, other arithmetic, turn(): weight = (rotation_slots < used).astype(jnp.float32)  20.8 us
    ppermute x8, starting transfers between devices, shifted(): return lax.ppermute(block, axis, route)  20.3 us
    gather x64, local copies, waits for them, and re-layouts, turn(): pos_win[:, second_blk]  18.5 us
    gather x64, local copies, waits for them, and re-layouts, turn(): bur_win[:, first_blk]  18.4 us
    gather x64, local copies, waits for them, and re-layouts, turn(): bur_win[:, second_blk]  18.4 us
  transfers between devices with their start and end apart: 16, of which 4 were waited for; matrix products, arithmetic and copies ran while one was open for 4% of the time, Pallas kernels for 0%

commit v1 on v0

--- a/solution.py
+++ b/solution.py
@@ -158,7 +158,10 @@
 
     def gather_moments(posit):
         local = block_moments(posit, burgers, block_cells, 16, width, 16 * my_slab)
-        summed = lax.psum(local, "dom")
+        peers_2, summed = (lax.axis_size("dom"), local)
+        for hop in [1 << k for k in range(peers_2.bit_length() - 1)]:
+            route_2 = [(i_2, i_2 ^ hop) for i_2 in range(peers_2)]
+            summed = summed + lax.ppermute(summed, "dom", route_2)
         return lax.all_gather(summed, "slab", axis=1, tiled=True)
 
     def speed(posit, window):

time: 327 us -> 317 us (0.969)
  blocking collectives: 52.4 us -> 31.3 us
  waiting for transfers between devices: 2.92 us -> 8.27 us
  starting transfers between devices: 41.6 us -> 46.8 us
    psum x2 -> x0, blocking collectives: 21.4 us -> none  [gather_moments(): summed = lax.psum(local, 'dom')]
    ppermute x0 -> x4, starting transfers between devices: none -> 6.17 us  [gather_moments(): summed = summed + lax.ppermute(summed, 'dom', route_2)]
    ppermute x0 -> x4, waiting for transfers between devices: none -> 5.73 us  [gather_moments(): summed = summed + lax.ppermute(summed, 'dom', route_2)]
  transfers between devices with their start and end apart: 16 -> 20, of which waited for: 4 -> 5; matrix products, arithmetic and copies ran while one was open for 4% -> 37% of each run, Pallas kernels for 0% -> 0%
where the time goes in v1:
time: 317 us; the launch traced here: 316 us
  other arithmetic  121 us (38%)
  local copies, waits for them, and re-layouts  94.8 us (30%)
  starting transfers between devices  46.8 us (15%)
  blocking collectives  31.3 us (10%)
  matrix products  8.84 us (3%)
  waiting for transfers between devices  8.27 us (3%)
    scatter-add x64, other arithmetic, turn(): return acc.at[:, first_blk].add(force_a).at[:, second_blk].add(force_b)  41.4 us
    all_gather x2, blocking collectives, gather_moments(): return lax.all_gather(summed, 'slab', axis=1, tiled=True)  31.3 us
    convert_element_type x32, other arithmetic, turn(): weight = (rotation_slots < used).astype(jnp.float32)  20.8 us
    ppermute x8, starting transfers between devices, shifted(): return lax.ppermute(block, axis, route)  20.3 us
    gather x64, local copies, waits for them, and re-layouts, turn(): pos_win[:, second_blk]  18.5 us
    gather x64, local copies, waits for them, and re-layouts, turn(): pos_win[:, first_blk]  18.4 us
    gather x64, local copies, waits for them, and re-layouts, turn(): bur_win[:, first_blk]  18.4 us
    gather x64, local copies, waits for them, and re-layouts, turn(): bur_win[:, second_blk]  18.4 us
  transfers between devices with their start and end apart: 20, of which 5 were waited for; matrix products, arithmetic and copies ran while one was open for 37% of the time, Pallas kernels for 0%

profile of v1, /device:TPU:0, one launch (start us, length us, event | category | flops | bytes accessed | tf_op | source)
XLA Modules:
  0.0 315.6 jit_solution(2632499617565949049)
XLA Ops:
  2.6 3.0 collective-permute-start.2
  8.3 3.0 collective-permute-start
  11.3 1.3 collective-permute-start.5
  12.6 4.5 %collective-permute-start.4 = (f32[6,3,1,512]{3,0,2,1:T(8,128)S(1)}, f32[6,3,1,512]{3,0,2,1:T(8,128)S(1)}, u32[]{:S(2)}, u32[]{:S(2)}) collective-permute-start(f32[6,3,1,512]{3,0,2,1:T(8,128)S(1)} %pad_maximum_fusion.4), channel_id=1, source_target_pairs={{0,1},{1,2},{2,3},{4,5},{5,6},{6,7},{8,9},{9,10},{10,11},{12,13},{... | collective-permute-start | bytes 110600 | tf_op jit(solution)/shard_map/ppermute | solution.py:22
  18.6 1.6 collective-permute-start.1
  20.3 105.3 %while.48 = (s32[]{:T(128)}, f32[3,36,128]{2,0,1:T(4,128)S(1)}, s32[]{:T(128)}, s32[64,2]{1,0:T(8,128)S(1)}, s32[]{:T(128)}, /*index=5*/s32[]{:T(128)}, s32[]{:T...) while((s32[]{:T(128)}, f32[3,36,128]{2,0,1:T(4,128)S(1)}, ...), condition=%wide.region_13.14_spmd, body=%wide.region_7.13_spmd.sunk | while | flops 2233267 | bytes 2855389 | solution.py:157
  125.7 1.3 collective-permute-start.6
  127.0 3.0 collective-permute-start.7
  130.1 14.0 %all_gather.6 = f32[39,128]{0,1:T(8,128)S(1)} all-gather(f32[39,16]{0,1:T(8,128)S(1)} %add.742), channel_id=1, replica_groups=mesh['slab'=8,'dom'=4] {'slab'}, dimensions={1}, use_global_device_ids=true | all-gather | bytes 22464 | tf_op jit(solution)/shard_map/all_gather | solution.py:165
  144.2 1.3 collective-permute-start.8
  145.5 4.5 %collective-permute-start.9 = (f32[3,512]{1,0:T(4,128)S(1)}, f32[3,512]{1,0:T(4,128)S(1)}, u32[]{:S(2)}, u32[]{:S(2)}) collective-permute-start(f32[3,512]{1,0:T(4,128)S(1)} %get-tuple-element.575), channel_id=1, source_target_pairs={{0,1},{1,2},{2,3},{4,5},{5,6},{6,7},{8,9},{9,10},{10,11},{12,13},{... | collective-permute-start | bytes 18440 | tf_op jit(solution)/shard_map/ppermute | solution.py:31
  150.1 5.3 %while.50 = (s32[]{:T(128)}, f32[3,512]{1,0:T(4,128)S(1)}, f32[3,512]{1,0:T(4,128)S(1)}, f32[2,3,64]{2,1,0:T(4,128)S(1)}, f32[2,39,64]{2,1,0:T(8,128)S(1)}, /*in...) while((s32[]{:T(128)}, f32[3,512]{1,0:T(4,128)S(1)}, f32[3,512]{1,0:T(4,128)S(1)}, ...), condition=%wide.region_6.7_spmd.clone, body=%wide.region_1.6_spmd.clone.sunk | while | flops 18023940 | bytes 6538151 | solution.py:82
  155.5 1.3 collective-permute-start.13
  156.8 3.0 collective-permute-start.12
  161.9 4.5 %collective-permute-start.14 = (f32[6,3,1,512]{3,0,2,1:T(8,128)S(1)}, f32[6,3,1,512]{3,0,2,1:T(8,128)S(1)}, u32[]{:S(2)}, u32[]{:S(2)}) collective-permute-start(f32[6,3,1,512]{3,0,2,1:T(8,128)S(1)} %pad_maximum_fusion.5), channel_id=1, source_target_pairs={{0,1},{1,2},{2,3},{4,5},{5,6},{6,7},{8,9},{9,10},{10,11},{12,13},{... | collective-permute-start | bytes 110600 | tf_op jit(solution)/shard_map/ppermute | solution.py:22
  167.1 1.3 collective-permute-done.14
  168.5 105.3 %while.49 = (s32[]{:T(128)}, f32[3,36,128]{2,0,1:T(4,128)S(1)}, s32[]{:T(128)}, s32[64,2]{1,0:T(8,128)S(1)}, s32[]{:T(128)}, /*index=5*/s32[]{:T(128)}, s32[]{:T...) while((s32[]{:T(128)}, f32[3,36,128]{2,0,1:T(4,128)S(1)}, ...), condition=%wide.region_27.28_spmd, body=%wide.region_21.27_spmd.sunk | while | flops 2233267 | bytes 2855389 | solution.py:157
  275.1 3.0 collective-permute-start.17
  278.4 3.7 %collective-permute-done.10 = f32[39,16]{0,1:T(8,128)S(1)} collective-permute-done((f32[39,16]{0,1:T(8,128)S(1)}, f32[39,16]{0,1:T(8,128)S(1)}, u32[]{:S(2)}, u32[]{:S(2)}) %collective-permute-start.10) | collective-permute-done | bytes 2528 | tf_op jit(solution)/shard_map/ppermute | solution.py:164
  282.1 1.6 collective-permute-start.11
  283.7 2.1 collective-permute-done.11
  285.7 17.3 %all_gather.7 = f32[39,128]{0,1:T(8,128)S(1)} all-gather(f32[39,16]{0,1:T(8,128)S(1)} %add.750), channel_id=1, replica_groups=mesh['slab'=8,'dom'=4] {'slab'}, dimensions={1}, use_global_device_ids=true | all-gather | bytes 22464 | tf_op jit(solution)/shard_map/all_gather | solution.py:165
  304.5 4.5 %collective-permute-start.19 = (f32[3,512]{1,0:T(4,128)S(1)}, f32[3,512]{1,0:T(4,128)S(1)}, u32[]{:S(2)}, u32[]{:S(2)}) collective-permute-start(f32[3,512]{1,0:T(4,128)S(1)} %get-tuple-element.573), channel_id=1, source_target_pairs={{0,1},{1,2},{2,3},{4,5},{5,6},{6,7},{8,9},{9,10},{10,11},{12,13},{... | collective-permute-start | bytes 18440 | tf_op jit(solution)/shard_map/ppermute | solution.py:31
  309.1 5.3 %while.51 = (s32[]{:T(128)}, f32[3,512]{1,0:T(4,128)S(1)}, f32[3,512]{1,0:T(4,128)S(1)}, f32[2,3,64]{2,1,0:T(4,128)S(1)}, f32[2,39,64]{2,1,0:T(8,128)S(1)}, /*in...) while((s32[]{:T(128)}, f32[3,512]{1,0:T(4,128)S(1)}, f32[3,512]{1,0:T(4,128)S(1)}, ...), condition=%wide.region_20.21_spmd.clone, body=%wide.region_15.20_spmd.clone.sunk | while | flops 18023940 | bytes 6538151 | solution.py:82
  (864 shorter events, 230.6 us)
Async XLA Ops:
  1.4 9.9 %collective-permute-start.3 = (f32[6,1,1,512]{3,0,2,1:T(8,128)S(1)}, f32[6,1,1,512]{3,0,2,1:T(8,128)S(1)}, u32[]{:S(2)}, u32[]{:S(2)}) collective-permute-start(f32[6,1,1,512]{3,0,2,1:T(8,128)S(1)} %fusion.138), channel_id=1, source_target_pairs={{4,0},{8,4},{12,8},{16,12},{20,16},{24,20},{28,24},{5,1},{9,5},{13... | collective-permute-start | bytes 36872 | tf_op jit(solution)/shard_map/ppermute | solution.py:23
  2.6 8.7 %collective-permute-start.2 = (f32[6,1,1,512]{3,0,2,1:T(8,128)S(1)}, f32[6,1,1,512]{3,0,2,1:T(8,128)S(1)}, u32[]{:S(2)}, u32[]{:S(2)}) collective-permute-start(f32[6,1,1,512]{3,0,2,1:T(8,128)S(1)} %fusion.138), channel_id=1, source_target_pairs={{0,4},{4,8},{8,12},{12,16},{16,20},{20,24},{24,28},{1,5},{5,9},{9,... | collective-permute-start | bytes 36872 | tf_op jit(solution)/shard_map/ppermute | solution.py:22
  8.3 10.3 %collective-permute-start = (f32[39,16]{0,1:T(8,128)S(1)}, f32[39,16]{0,1:T(8,128)S(1)}, u32[]{:S(2)}, u32[]{:S(2)}) collective-permute-start(f32[39,16]{0,1:T(8,128)S(1)} %fusion.151), channel_id=1, source_target_pairs={{0,1},{1,0},{2,3},{3,2},{4,5},{5,4},{6,7},{7,6},{8,9},{9,8},{10,11... | collective-permute-start | bytes 7496 | tf_op jit(solution)/shard_map/ppermute | solution.py:164
  11.3 8.9 %collective-permute-start.5 = (f32[6,3,1,512]{3,0,2,1:T(8,128)S(1)}, f32[6,3,1,512]{3,0,2,1:T(8,128)S(1)}, u32[]{:S(2)}, u32[]{:S(2)}) collective-permute-start(f32[6,3,1,512]{3,0,2,1:T(8,128)S(1)} %pad_maximum_fusion.4), channel_id=1, source_target_pairs={{1,0},{2,1},{3,2},{5,4},{6,5},{7,6},{9,8},{10,9},{11,10},{13,12},{... | collective-permute-start | bytes 110600 | tf_op jit(solution)/shard_map/ppermute | solution.py:23
  12.6 7.6 %collective-permute-start.4 = (f32[6,3,1,512]{3,0,2,1:T(8,128)S(1)}, f32[6,3,1,512]{3,0,2,1:T(8,128)S(1)}, u32[]{:S(2)}, u32[]{:S(2)}) collective-permute-start(f32[6,3,1,512]{3,0,2,1:T(8,128)S(1)} %pad_maximum_fusion.4), channel_id=1, source_target_pairs={{0,1},{1,2},{2,3},{4,5},{5,6},{6,7},{8,9},{9,10},{10,11},{12,13},{... | collective-permute-start | bytes 110600 | tf_op jit(solution)/shard_map/ppermute | solution.py:22
  18.6 111.4 %collective-permute-start.1 = (f32[39,16]{0,1:T(8,128)S(1)}, f32[39,16]{0,1:T(8,128)S(1)}, u32[]{:S(2)}, u32[]{:S(2)}) collective-permute-start(f32[39,16]{0,1:T(8,128)S(1)} %add.741), channel_id=1, source_target_pairs={{0,2},{1,3},{2,0},{3,1},{4,6},{5,7},{6,4},{7,5},{8,10},{9,11},{10,... | collective-permute-start | bytes 7496 | tf_op jit(solution)/shard_map/ppermute | solution.py:164
  20.3 129.7 %copy-start = (f32[3,512]{1,0:T(4,128)S(1)}, f32[3,512]{1,0:T(4,128)}, u32[]{:S(2)}) copy-start(f32[3,512]{1,0:T(4,128)} %param.15) | copy-start | bytes 18436
  20.3 129.7 %copy-start.1 = (f32[3,512]{1,0:T(4,128)S(1)}, f32[3,512]{1,0:T(4,128)}, u32[]{:S(2)}) copy-start(f32[3,512]{1,0:T(4,128)} %param.14) | copy-start | bytes 18436
  125.7 18.5 %collective-permute-start.6 = (f32[3,3,512]{2,0,1:T(4,128)S(1)}, f32[3,3,512]{2,0,1:T(4,128)S(1)}, u32[]{:S(2)}, u32[]{:S(2)}) collective-permute-start(f32[3,3,512]{2,0,1:T(4,128)S(1)} %get-tuple-element.570), channel_id=1, source_target_pairs={{4,0},{8,4},{12,8},{16,12},{20,16},{24,20},{28,24},{5,1},{9,5},{13... | collective-permute-start | bytes 55304 | tf_op jit(solution)/shard_map/ppermute | solution.py:31
  127.0 17.2 %collective-permute-start.7 = (f32[3,3,512]{2,0,1:T(4,128)S(1)}, f32[3,3,512]{2,0,1:T(4,128)S(1)}, u32[]{:S(2)}, u32[]{:S(2)}) collective-permute-start(f32[3,3,512]{2,0,1:T(4,128)S(1)} %get-tuple-element.571), channel_id=1, source_target_pairs={{0,4},{4,8},{8,12},{12,16},{16,20},{20,24},{24,28},{1,5},{5,9},{9,... | collective-permute-start | bytes 55304 | tf_op jit(solution)/shard_map/ppermute | solution.py:31
  144.2 11.2 %collective-permute-start.8 = (f32[3,512]{1,0:T(4,128)S(1)}, f32[3,512]{1,0:T(4,128)S(1)}, u32[]{:S(2)}, u32[]{:S(2)}) collective-permute-start(f32[3,512]{1,0:T(4,128)S(1)} %get-tuple-element.574), channel_id=1, source_target_pairs={{1,0},{2,1},{3,2},{5,4},{6,5},{7,6},{9,8},{10,9},{11,10},{13,12},{... | collective-permute-start | bytes 18440 | tf_op jit(solution)/shard_map/ppermute | solution.py:31
  145.5 9.9 %collective-permute-start.9 = (f32[3,512]{1,0:T(4,128)S(1)}, f32[3,512]{1,0:T(4,128)S(1)}, u32[]{:S(2)}, u32[]{:S(2)}) collective-permute-start(f32[3,512]{1,0:T(4,128)S(1)} %get-tuple-element.575), channel_id=1, source_target_pairs={{0,1},{1,2},{2,3},{4,5},{5,6},{6,7},{8,9},{9,10},{10,11},{12,13},{... | collective-permute-start | bytes 18440 | tf_op jit(solution)/shard_map/ppermute | solution.py:31
  150.1 5.3 %copy-start.2 = (f32[512]{0:T(512)S(1)}, f32[512]{0:T(512)}, u32[]{:S(2)}) copy-start(f32[512]{0:T(512)} %param.16) | copy-start | bytes 6148
  155.5 4.4 %collective-permute-start.13 = (f32[6,1,1,512]{3,0,2,1:T(8,128)S(1)}, f32[6,1,1,512]{3,0,2,1:T(8,128)S(1)}, u32[]{:S(2)}, u32[]{:S(2)}) collective-permute-start(f32[6,1,1,512]{3,0,2,1:T(8,128)S(1)} %fusion.139), channel_id=1, source_target_pairs={{4,0},{8,4},{12,8},{16,12},{20,16},{24,20},{28,24},{5,1},{9,5},{13... | collective-permute-start | bytes 36872 | tf_op jit(solution)/shard_map/ppermute | solution.py:23
  156.8 3.9 %collective-permute-start.12 = (f32[6,1,1,512]{3,0,2,1:T(8,128)S(1)}, f32[6,1,1,512]{3,0,2,1:T(8,128)S(1)}, u32[]{:S(2)}, u32[]{:S(2)}) collective-permute-start(f32[6,1,1,512]{3,0,2,1:T(8,128)S(1)} %fusion.139), channel_id=1, source_target_pairs={{0,4},{4,8},{8,12},{12,16},{16,20},{20,24},{24,28},{1,5},{5,9},{9,... | collective-permute-start | bytes 36872 | tf_op jit(solution)/shard_map/ppermute | solution.py:22
  160.6 6.4 %collective-permute-start.15 = (f32[6,3,1,512]{3,0,2,1:T(8,128)S(1)}, f32[6,3,1,512]{3,0,2,1:T(8,128)S(1)}, u32[]{:S(2)}, u32[]{:S(2)}) collective-permute-start(f32[6,3,1,512]{3,0,2,1:T(8,128)S(1)} %pad_maximum_fusion.5), channel_id=1, source_target_pairs={{1,0},{2,1},{3,2},{5,4},{6,5},{7,6},{9,8},{10,9},{11,10},{13,12},{... | collective-permute-start | bytes 110600 | tf_op jit(solution)/shard_map/ppermute | solution.py:23
  161.9 6.5 %collective-permute-start.14 = (f32[6,3,1,512]{3,0,2,1:T(8,128)S(1)}, f32[6,3,1,512]{3,0,2,1:T(8,128)S(1)}, u32[]{:S(2)}, u32[]{:S(2)}) collective-permute-start(f32[6,3,1,512]{3,0,2,1:T(8,128)S(1)} %pad_maximum_fusion.5), channel_id=1, source_target_pairs={{0,1},{1,2},{2,3},{4,5},{5,6},{6,7},{8,9},{9,10},{10,11},{12,13},{... | collective-permute-start | bytes 110600 | tf_op jit(solution)/shard_map/ppermute | solution.py:22
  273.8 29.4 %collective-permute-start.16 = (f32[3,3,512]{2,0,1:T(4,128)S(1)}, f32[3,3,512]{2,0,1:T(4,128)S(1)}, u32[]{:S(2)}, u32[]{:S(2)}) collective-permute-start(f32[3,3,512]{2,0,1:T(4,128)S(1)} %get-tuple-element.568), channel_id=1, source_target_pairs={{4,0},{8,4},{12,8},{16,12},{20,16},{24,20},{28,24},{5,1},{9,5},{13... | collective-permute-start | bytes 55304 | tf_op jit(solution)/shard_map/ppermute | solution.py:31
  275.1 28.1 %collective-permute-start.17 = (f32[3,3,512]{2,0,1:T(4,128)S(1)}, f32[3,3,512]{2,0,1:T(4,128)S(1)}, u32[]{:S(2)}, u32[]{:S(2)}) collective-permute-start(f32[3,3,512]{2,0,1:T(4,128)S(1)} %get-tuple-element.569), channel_id=1, source_target_pairs={{0,4},{4,8},{8,12},{12,16},{16,20},{20,24},{24,28},{1,5},{5,9},{9,... | collective-permute-start | bytes 55304 | tf_op jit(solution)/shard_map/ppermute | solution.py:31
  278.4 3.7 %collective-permute-start.10 = (f32[39,16]{0,1:T(8,128)S(1)}, f32[39,16]{0,1:T(8,128)S(1)}, u32[]{:S(2)}, u32[]{:S(2)}) collective-permute-start(f32[39,16]{0,1:T(8,128)S(1)} %fusion.150), channel_id=1, source_target_pairs={{0,1},{1,0},{2,3},{3,2},{4,5},{5,4},{6,7},{7,6},{8,9},{9,8},{10,11... | collective-permute-start | bytes 7496 | tf_op jit(solution)/shard_map/ppermute | solution.py:164
  282.1 3.7 %collective-permute-start.11 = (f32[39,16]{0,1:T(8,128)S(1)}, f32[39,16]{0,1:T(8,128)S(1)}, u32[]{:S(2)}, u32[]{:S(2)}) collective-permute-start(f32[39,16]{0,1:T(8,128)S(1)} %add.749), channel_id=1, source_target_pairs={{0,2},{1,3},{2,0},{3,1},{4,6},{5,7},{6,4},{7,5},{8,10},{9,11},{10,... | collective-permute-start | bytes 7496 | tf_op jit(solution)/shard_map/ppermute | solution.py:164
  303.2 11.2 %collective-permute-start.18 = (f32[3,512]{1,0:T(4,128)S(1)}, f32[3,512]{1,0:T(4,128)S(1)}, u32[]{:S(2)}, u32[]{:S(2)}) collective-permute-start(f32[3,512]{1,0:T(4,128)S(1)} %get-tuple-element.572), channel_id=1, source_target_pairs={{1,0},{2,1},{3,2},{5,4},{6,5},{7,6},{9,8},{10,9},{11,10},{13,12},{... | collective-permute-start | bytes 18440 | tf_op jit(solution)/shard_map/ppermute | solution.py:31
  304.5 9.9 %collective-permute-start.19 = (f32[3,512]{1,0:T(4,128)S(1)}, f32[3,512]{1,0:T(4,128)S(1)}, u32[]{:S(2)}, u32[]{:S(2)}) collective-permute-start(f32[3,512]{1,0:T(4,128)S(1)} %get-tuple-element.573), channel_id=1, source_target_pairs={{0,1},{1,2},{2,3},{4,5},{5,6},{6,7},{8,9},{9,10},{10,11},{12,13},{... | collective-permute-start | bytes 18440 | tf_op jit(solution)/shard_map/ppermute | solution.py:31
